TPU v7x, 32 devices: a whole 2x2x4 slice. The times are simulated.
32 devices in a mesh: ctx: 16 (over z, y, core), sec: 2 (over x).
Axes of the slice: x: 2, y: 2, z: 4, core: 2. Of those that a mesh axis runs over, the one named last changes fastest.
Arguments:
- queries: bfloat16 [1024, 6144], P('ctx', 'sec'), may hold values from -128 to 128
- keys: bfloat16 [1280, 1024], P('ctx', 'sec'), may hold values from -8 to 8
- values: bfloat16 [1280, 1024], P('ctx', 'sec'), may hold values from -6 to 6
- gain: float32 [6144], P('sec'), may hold values from 0.5 to 1.5
- router: float32 [6144, 8], P('sec'), may hold values from -0.078125 to 0.078125
- w_gate: bfloat16 [6144, 16384], P('sec', 'ctx'), may hold values from -0.078125 to 0.078125
- w_up: bfloat16 [6144, 16384], P('sec', 'ctx'), may hold values from -0.078125 to 0.078125
- w_down: bfloat16 [16384, 6144], P('ctx', 'sec'), may hold values from -0.125 to 0.125
- routes: int32 [1024, 2], P('ctx'), may hold values from 0 to 7, all different within a row; in each aligned block of 64 rows (0 to 63, 64 to 127, ...) at most 20 rows name the same one
Outputs:
- normed: bfloat16 [1024, 6144], P('ctx', 'sec')
- moe_out: bfloat16 [1024, 6144], P('ctx', 'sec')
Inputs may be any that keep to these rules, and one draw needn't show every extreme that they name: `routes`: each row names 2 different experts. Among the rows at one index of ctx no expert is named more than 20 times, and in every draw some expert is named exactly 20 times there.
All inputs are finite; a program needn't handle non-finite values.
Results may differ from a plain program's by a relative error of at most 0.023.
Values may be sent and summed in bfloat16 or wider, within the bound.
A program may use at most 192 MiB of HBM per device.

v0:
```python
import math

import jax
import jax.numpy as jnp
from jax import lax
from jax.sharding import PartitionSpec as P

D = 6144
HEADS = 48
KV_HEADS = 8
HEAD_DIM = 128
EXPERTS = 8
TOP = 2
CAP = 20


def on_device(queries, keys, values, gain, router, w_gate, w_up, w_down, routes):
    cycle_size = lax.axis_size("ctx")
    token_count = queries.shape[0]
    kv_rows = keys.shape[0]
    cache = (kv_rows - token_count) * cycle_size
    query_pos = (
        cache + lax.axis_index("ctx") * token_count + jnp.arange(token_count, dtype=jnp.int32)
    )
    kv_local = keys.shape[1] // HEAD_DIM
    group_size = HEADS // KV_HEADS
    query_heads = queries.reshape(token_count, kv_local, group_size, HEAD_DIM)
    scale_factor = 1.0 / math.sqrt(HEAD_DIM)
    pieces = (
        lax.all_gather(keys, "ctx", axis=0, tiled=True),
        lax.all_gather(values, "ctx", axis=0, tiled=True),
    )
    running = jnp.full((kv_local, group_size, token_count), -1e30, jnp.float32)
    key_piece = pieces[0].reshape(pieces[0].shape[0], kv_local, HEAD_DIM)
    value_piece = pieces[1].reshape(pieces[1].shape[0], kv_local, HEAD_DIM)
    key_pos = jnp.arange(key_piece.shape[0], dtype=jnp.int32)
    visible = key_pos[None, :] <= query_pos[:, None]
    scores = (
        jnp.einsum("tgqd,ngd->gqtn", query_heads, key_piece, preferred_element_type=jnp.float32)
        * scale_factor
    )
    scores = jnp.where(visible, scores, -1e30)
    newest = jnp.maximum(running, jnp.max(scores, axis=3))
    weights = jnp.where(visible, jnp.exp(scores - newest[..., None]), 0.0)
    total = jnp.sum(weights, axis=3)
    mixed = jnp.einsum(
        "gqtn,ngd->gqtd",
        weights.astype(jnp.bfloat16),
        value_piece,
        preferred_element_type=jnp.float32,
    )
    accum = mixed
    running, total, accum = (newest, total, accum)
    attended = (
        (accum / total[..., None])
        .transpose(2, 0, 1, 3)
        .reshape(token_count, kv_local * group_size * HEAD_DIM)
    )
    attended = attended.astype(jnp.bfloat16)
    attn_float = attended.astype(jnp.float32)
    gained = attn_float * gain[None, :]
    part_squares = jnp.sum(attn_float * attn_float, axis=1)
    part_logits = jnp.dot(gained, router, precision=lax.Precision.HIGHEST)
    squares, logits = lax.psum((part_squares, part_logits), "sec")
    factor = lax.rsqrt(squares / D + 1e-05)
    normed = (gained * factor[:, None]).astype(jnp.bfloat16)
    logits = logits * factor[:, None]
    expert_ids = jnp.arange(EXPERTS, dtype=jnp.int32)
    picks = (routes[:, :, None] == expert_ids[None, None, :]).astype(jnp.float32)
    chosen = jnp.sum(picks * logits[:, None, :], axis=2)
    combine = 1.0 / jnp.sum(jnp.exp(chosen[:, None, :] - chosen[:, :, None]), axis=2)
    flat_routes = routes.reshape(token_count * TOP)
    hot = (flat_routes[:, None] == expert_ids[None, :]).astype(jnp.int32)
    before = jnp.cumsum(hot, axis=0) - hot
    slots = jnp.sum(before * hot, axis=1)
    cells = flat_routes * CAP + slots
    placing = (cells[:, None] == jnp.arange(EXPERTS * CAP, dtype=jnp.int32)[None, :]).astype(
        jnp.float32
    )
    placing = placing.reshape(token_count, TOP, EXPERTS * CAP)
    token_place = jnp.sum(placing, axis=1).astype(jnp.bfloat16)
    width_local = normed.shape[1]
    packed = jnp.einsum(
        "tc,td->cd", token_place, normed, preferred_element_type=jnp.float32
    ).astype(jnp.bfloat16)
    group_count = cycle_size // EXPERTS
    outgoing = jnp.broadcast_to(
        packed.reshape(EXPERTS, 1, CAP, width_local), (EXPERTS, group_count, CAP, width_local)
    )
    outgoing = outgoing.reshape(cycle_size, CAP, width_local)
    received = lax.all_to_all(outgoing, "ctx", split_axis=0, concat_axis=0, tiled=True)
    gate_part = jnp.einsum("sid,df->sif", received, w_gate, preferred_element_type=jnp.float32)
    up_part = jnp.einsum("sid,df->sif", received, w_up, preferred_element_type=jnp.float32)
    gate_full = lax.psum(gate_part.astype(jnp.bfloat16), "sec").astype(jnp.float32)
    up_full = lax.psum(up_part.astype(jnp.bfloat16), "sec").astype(jnp.float32)
    hidden = (jax.nn.silu(gate_full) * up_full).astype(jnp.bfloat16)
    down_part = jnp.einsum(
        "sif,fd->sid", hidden, w_down, preferred_element_type=jnp.float32
    ).astype(jnp.bfloat16)
    returned = lax.all_to_all(down_part, "ctx", split_axis=0, concat_axis=0, tiled=True)
    summed = jnp.sum(
        returned.reshape(EXPERTS, group_count, CAP, width_local).astype(jnp.float32), axis=1
    )
    summed = summed.reshape(EXPERTS * CAP, width_local)
    mixing = jnp.sum(placing * combine[:, :, None], axis=1)
    moe_out = jnp.dot(mixing, summed, precision=lax.Precision.HIGHEST).astype(jnp.bfloat16)
    return (normed, moe_out)


def solution(mesh):
    in_specs = (
        P("ctx", "sec"),
        P("ctx", "sec"),
        P("ctx", "sec"),
        P("sec"),
        P("sec", None),
        P("sec", "ctx"),
        P("sec", "ctx"),
        P("ctx", "sec"),
        P("ctx", None),
    )
    out_specs = (P("ctx", "sec"), P("ctx", "sec"))
    return jax.shard_map(
        on_device, mesh=mesh, in_specs=in_specs, out_specs=out_specs, check_vma=False
    )
```

profile of v0, /device:TPU:9, one launch (start us, length us, event | category | flops | bytes accessed | tf_op | source)
XLA Modules:
  0.0 300.7 jit_solution(6938706483187099072)
XLA Ops:
  7.2 0.0 copy-start
  7.2 0.0 all-gather.3.cloned.1.call-start
  7.2 0.7 all-gather.3.cloned.1.call-update
  7.9 0.0 all-gather.5.cloned.1.call-start
  8.0 0.7 all-gather.5.cloned.1.call-update
  8.7 0.0 all-reduce.4.cloned.1.call-start
  8.7 1.5 reshape.65
  10.2 0.8 copy.55
  11.0 0.1 eq.42
  11.1 0.1 fusion.45
  11.2 0.2 reduce_window_sum.11
  11.4 0.2 select_reduce_fusion.1
  11.6 0.1 reduce_sum.77
  11.7 0.1 copy.56
  11.8 0.7 multiply_add_fusion
  12.5 0.1 iota_compare_fusion
  12.6 37.2 %all-gather.3.cloned.1.call-done = bf16[1280,512]{1,0:T(8,128)(2,1)} async-done(((bf16[80,512]{1,0:T(8,128)(2,1)}), bf16[1280,512]{1,0:T(8,128)(2,1)}) %all-gather.3.cloned.1.call-update) | async-done | bytes 1310736 | tf_op jit(solution)/shard_map/all_gather | solution.py:30
  49.8 1.6 copy.49
  51.4 1.6 fusion
  53.0 0.0 copy-start.1
  53.0 3.1 %copy-done.1 = f32[4,1280,64,6]{1,2,3,0:T(8,128)} copy-done((f32[4,1280,64,6]{1,2,3,0:T(8,128)}, f32[4,1280,64,6]{1,2,3,0:T(8,128)S(1)}, u32[]{:S(2)}) %copy-start.1) | copy-done | bytes 7864344
  56.1 2.4 fusion.7
  58.5 31.2 %all-gather.5.cloned.1.call-done = bf16[1280,512]{1,0:T(8,128)(2,1)} async-done(((bf16[80,512]{1,0:T(8,128)(2,1)}), bf16[1280,512]{1,0:T(8,128)(2,1)}) %all-gather.5.cloned.1.call-update) | async-done | bytes 1310736 | tf_op jit(solution)/shard_map/all_gather | solution.py:31
  89.7 1.6 copy.52
  91.3 4.4 %multiply_reduce_fusion = (f32[64]{0:T(128)S(1)}, f32[64,4,6,128]{3,0,2,1:T(8,128)S(1)}) fusion(f32[64,4,6]{0,2,1:T(8,128)S(1)} %bitcast.71, bf16[1280,4,128,1]{0,2,3,1:T(8,128)(2,1)S(1)} %bitcast.70, f32[4,1280,64,6]{1,2,3,0:T(8,128)} %copy-done.1, f32[4,6,64]{2,1,0:T(8,128)S(1)} %broadcast_maximum_fusion, pred[64,1280]{1,0:T(8,128)(4,1)S(1)} %iota_compare_fusion), kind=kOutput, calls=%fused_computation.32 | convolution fusion | flops 514129856 | bytes 10055936 | tf_op jit(solution)/shard_map/gqtn,ngd->gqtd/dot_general | solution.py:46
  95.8 0.0 copy-start.3
  95.8 0.5 copy.54
  96.3 0.0 copy-start.4
  96.3 0.2 reshape.69
  96.5 0.0 copy-done
  96.5 0.0 copy-done.3
  96.5 0.7 fusion.40
  97.2 3.8 %all-reduce = (f32[64]{0:T(128)S(1)}, f32[64,8]{0,1:T(8,128)S(1)}) all-reduce(f32[64]{0:T(128)S(1)} %get-tuple-element.10, f32[64,8]{0,1:T(8,128)S(1)} %fusion.40), channel_id=1, replica_groups=mesh['ctx'=16,'sec'=2] {'sec'}, use_global_device_ids=true, to_apply=%region_3.4 | all-reduce | flops 576 | bytes 4608 | tf_op jit(solution)/shard_map/psum | solution.py:64
  101.0 0.1 multiply_convert_fusion
  101.2 0.0 copy-start.2
  101.2 0.0 copy-done.4
  101.3 0.1 convert_reduce_fusion.1
  101.4 0.4 convolution_convert_fusion
  101.8 0.3 broadcast_in_dim.22
  102.1 0.3 broadcast_in_dim.23
  102.4 0.0 copy-done.2
  102.4 0.0 slice-start
  102.4 59.6 %all_to_all.10 = bf16[16,20,3072]{2,1,0:T(8,128)(2,1)S(1)} all-to-all(bf16[16,20,3072]{2,1,0:T(8,128)(2,1)S(1)} %bitcast.68), channel_id=1, replica_groups=mesh['ctx'=16,'sec'=2] {'ctx'}, dimensions={0} | all-to-all | bytes 3932160 | tf_op jit(solution)/shard_map/all_to_all | solution.py:91
  162.0 0.0 slice-start.1
  162.1 6.5 %fusion.20 = bf16[16,20,1024]{2,1,0:T(8,128)(2,1)} fusion(bf16[16,20,3072]{2,1,0:T(8,128)(2,1)S(1)} %all_to_all.10, bf16[3072,1024]{1,0:T(8,128)(2,1)} %param.14), kind=kOutput, calls=%fused_computation.24 | convolution fusion | flops 2013593600 | bytes 8912896 | tf_op jit(solution)/shard_map/sid,df->sif/dot_general | solution.py:92
  168.5 0.0 slice-done
  168.5 0.0 slice-done.1
  168.5 3.6 %fusion.23 = bf16[16,20,1024]{2,1,0:T(8,128)(2,1)} fusion(bf16[16,20,3072]{2,1,0:T(8,128)(2,1)S(1)} %all_to_all.10, bf16[3072,1024]{1,0:T(8,128)(2,1)S(1)} %bitcast.73), kind=kOutput, calls=%fused_computation.25 | convolution fusion | flops 2013593600 | bytes 8912896 | tf_op jit(solution)/shard_map/sid,df->sif/dot_general | solution.py:93
  172.1 0.0 all-reduce.4.cloned.1.call-update
  172.1 50.7 %all-reduce.4.cloned.1.call-done = (bf16[16,20,1024]{2,1,0:T(8,128)(2,1)}, bf16[16,20,1024]{2,1,0:T(8,128)(2,1)}) async-done(((bf16[16,20,1024]{2,1,0:T(8,128)(2,1)}, bf16[16,20,1024]{2,1,0:T(8,128)(2,1)}), (bf16[16,20,1024]{2,1,0:T(8,128)(2,1)}, bf16[16,20,1024]{2,1,0:T(8,128)(2,1)})) %all-reduce.4.cloned.1.call-update) | async-done | bytes 1310736 | tf_op jit(solution)/shard_map/psum | solution.py:95
  222.9 6.1 %fusion.9 = bf16[16,20,3072]{2,1,0:T(8,128)(2,1)S(1)} fusion(bf16[1024,3072]{1,0:T(8,128)(2,1)} %param.16, bf16[16,20,1024]{2,1,0:T(8,128)(2,1)} %get-tuple-element.6, bf16[16,20,1024]{2,1,0:T(8,128)(2,1)} %get-tuple-element.7), kind=kOutput, calls=%fused_computation.12 | convolution fusion | flops 2016870400 | bytes 9568256 | tf_op jit(solution)/shard_map/sif,fd->sid/dot_general | solution.py:97
  229.0 59.8 %all_to_all.11 = bf16[16,20,3072]{2,1,0:T(8,128)(2,1)S(1)} all-to-all(bf16[16,20,3072]{2,1,0:T(8,128)(2,1)S(1)} %fusion.9), channel_id=1, replica_groups=mesh['ctx'=16,'sec'=2] {'ctx'}, dimensions={0} | all-to-all | bytes 3932160 | tf_op jit(solution)/shard_map/all_to_all | solution.py:100
  288.8 0.5 convert_reduce_fusion
  289.3 1.4 reshape.68
  290.7 3.4 %convolution_convert_fusion.1 = bf16[64,3072]{1,0:T(8,128)(2,1)} fusion(f32[64,160]{1,0:T(8,128)S(1)} %get-tuple-element.3, f32[160,3072]{1,0:T(8,128)} %reshape.68), kind=kOutput, calls=%fused_computation.16 | convolution fusion | flops 377683968 | bytes 2400256 | tf_op jit(solution)/shard_map/dot_general | solution.py:106
  (8 shorter events, 0.1 us)
Async XLA Ops:
  7.2 89.3 %copy-start = (f32[3072,8]{0,1:T(8,128)S(1)}, f32[3072,8]{0,1:T(8,128)}, u32[]{:S(2)}) copy-start(f32[3072,8]{0,1:T(8,128)} %param.13) | copy-start | bytes 294916
  7.2 42.6 %all-gather.3.cloned.1.call-start = ((), (), s32[]{:S(2)}) async-start(), calls=%async_computation.2 | async-start | bytes 1392640 | tf_op jit(solution)/shard_map/all_gather | solution.py:30
  7.9 81.8 %all-gather.5.cloned.1.call-start = ((), (), s32[]{:S(2)}) async-start(), calls=%async_computation.3 | async-start | bytes 1392640 | tf_op jit(solution)/shard_map/all_gather | solution.py:31
  8.7 214.2 %all-reduce.4.cloned.1.call-start = ((), (), s32[]{:S(2)}) async-start(), calls=%async_computation.4 | async-start | bytes 3145728 | tf_op jit(solution)/shard_map/psum | solution.py:95
  53.0 3.1 %copy-start.1 = (f32[4,1280,64,6]{1,2,3,0:T(8,128)}, f32[4,1280,64,6]{1,2,3,0:T(8,128)S(1)}, u32[]{:S(2)}) copy-start(f32[4,1280,64,6]{1,2,3,0:T(8,128)S(1)} %get-tuple-element.9) | copy-start | bytes 23592964
  95.8 0.7 copy-start.3
  96.3 5.0 %copy-start.4 = (s32[64,2]{0,1:T(2,128)S(1)}, s32[64,2]{0,1:T(2,128)}, u32[]{:S(2)}) copy-start(s32[64,2]{0,1:T(2,128)} %param.17) | copy-start | bytes 1540
  101.2 1.2 copy-start.2
  102.4 66.1 %slice-start = ((s8[6291456]{0:T(1024)(128)(4,1)}), s8[4194304]{0:T(1024)(128)(4,1)S(1)}, s32[]{:S(2)}) async-start(s8[6291456]{0:T(1024)(128)(4,1)} %bitcast.72), calls=%async_computation.5 | async-start | bytes 8388608
  162.0 6.5 %slice-start.1 = ((s8[6291456]{0:T(1024)(128)(4,1)}), s8[2097152]{0:T(1024)(128)(4,1)S(1)}, s32[]{:S(2)}) async-start(s8[6291456]{0:T(1024)(128)(4,1)} %bitcast.72), calls=%async_computation.6 | async-start | bytes 4194304
Sparse Core Ops, SparseCore 0:
  10.3 39.4 all-gather.2
  52.1 37.6 all-gather.4
  172.2 50.5 all-reduce.3
where the time goes:
time: 303 us; the launch traced here: 301 us
  blocking collectives  123 us (41%)
  waiting for transfers between devices  121 us (40%)
  matrix products  26.8 us (9%)
  between operations  14 us (5%)
  local copies, waits for them, and re-layouts  11.5 us (4%)
  other arithmetic  4.43 us (1%)
    all_to_all x1, blocking collectives, on_device(): lax.all_to_all(down_part, 'ctx', split_axis=0, concat_axis=0, tiled=True)  59.8 us
    all_to_all x1, blocking collectives, on_device(): lax.all_to_all(outgoing, 'ctx', split_axis=0, concat_axis=0, tiled=True)  59.6 us
    psum x1, waiting for transfers between devices, on_device(): up_full = lax.psum(up_part.astype(jnp.bfloat16), 'sec').astype(jnp.float32)  50.7 us
    all_gather x1, waiting for transfers between devices, on_device(): lax.all_gather(keys, 'ctx', axis=0, tiled=True)  37.2 us
    all_gather x1, waiting for transfers between devices, on_device(): lax.all_gather(values, 'ctx', axis=0, tiled=True)  31.2 us
    dot_general x1, matrix products, on_device(): jnp.einsum('sid,df->sif', received, w_gate, preferred_element_type=jnp.fl...  6.47 us
    dot_general x1, matrix products, on_device(): jnp.einsum('sif,fd->sid', hidden, w_down, preferred_element_type=jnp.floa...  6.11 us
  transfers between devices with their start and end apart: 3, of which 3 were waited for; matrix products, arithmetic and copies ran while one was open for 3% of the time, Pallas kernels for 0%

commit v1 on v0

--- a/solution.py
+++ b/solution.py
@@ -1,8 +1,12 @@
+import functools
 import math
 
 import jax
 import jax.numpy as jnp
+import numpy as np
 from jax import lax
+from jax.experimental import pallas as pl
+from jax.experimental.pallas import tpu as pltpu
 from jax.sharding import PartitionSpec as P
 
 D = 6144
@@ -12,51 +16,415 @@
 EXPERTS = 8
 TOP = 2
 CAP = 20
+SPLIT = 4
+UNIT = CAP * SPLIT
+CHUNKS = 2
+PAIR = 4
+MESH = pl.DeviceIdType.MESH
+
+
+def on_ctx(index):
+    return {"ctx": index}
+
+
+def attend_kernel(n, q_hbm, k_hbm, v_hbm, out_ref, q_ref, kv, local_sem, z_send, y_send, c_send, recv):
+    me = lax.axis_index("ctx")
+    far = n // 4
+    zi, yi, ci = me // 4, (me // 2) % 2, me % 2
+    rows = k_hbm.shape[0]
+
+    def slot(source):
+        return kv.at[:, pl.ds(pl.multiple_of(source * rows, 16), rows), :]
+
+    mine = pl.ds(pl.multiple_of(me * rows, 16), rows)
+    loads = [
+        pltpu.make_async_copy(k_hbm, kv.at[0, mine, :], local_sem.at[0]),
+        pltpu.make_async_copy(v_hbm, kv.at[1, mine, :], local_sem.at[1]),
+        pltpu.make_async_copy(q_hbm, q_ref, local_sem.at[2]),
+    ]
+    for load in loads:
+        load.start()
+    y_peer = zi * 4 + (1 - yi) * 2 + ci
+    c_peer = zi * 4 + yi * 2 + 1 - ci
+    barrier = pltpu.get_barrier_semaphore()
+    for k in range(1, far):
+        pl.semaphore_signal(
+            barrier, inc=1, device_id=on_ctx(((zi + k) % far) * 4 + yi * 2 + ci), device_id_type=MESH
+        )
+    for peer in (y_peer, c_peer):
+        pl.semaphore_signal(barrier, inc=1, device_id=on_ctx(peer), device_id_type=MESH)
+    pl.semaphore_wait(barrier, far + 1)
+    loads[0].wait()
+    loads[1].wait()
+    sent = []
+
+    def send(source, peer, sem):
+        copy = pltpu.make_async_remote_copy(
+            src_ref=slot(source), dst_ref=slot(source), send_sem=sem, recv_sem=recv.at[source],
+            device_id=on_ctx(peer), device_id_type=MESH,
+        )
+        copy.start()
+        sent.append(copy)
+
+    def arrived(source):
+        pltpu.make_async_remote_copy(
+            src_ref=slot(source), dst_ref=slot(source), send_sem=c_send.at[0], recv_sem=recv.at[source],
+            device_id=on_ctx(c_peer), device_id_type=MESH,
+        ).wait_recv()
+
+    for k in range(1, far):
+        send(me, ((zi + k) % far) * 4 + yi * 2 + ci, z_send.at[k - 1])
+    send(me, y_peer, y_send.at[0])
+    send(me, c_peer, c_send.at[0])
+    for k in range(1, far):
+        source = ((zi + far - k) % far) * 4 + yi * 2 + ci
+        arrived(source)
+        send(source, y_peer, y_send.at[k])
+        send(source, c_peer, c_send.at[k])
+    for k in range(far):
+        source = ((zi + far - k) % far) * 4 + (1 - yi) * 2 + ci
+        arrived(source)
+        send(source, c_peer, c_send.at[far + k])
+    for k in range(far):
+        for y in range(2):
+            arrived(((zi + far - k) % far) * 4 + y * 2 + 1 - ci)
+    loads[2].wait()
+
+    tokens = q_ref.shape[0]
+    group = HEADS // KV_HEADS
+    length = n * rows
+    position = (rows - tokens) * n + me * tokens + lax.broadcasted_iota(jnp.int32, (tokens, length), 0)
+    visible = lax.broadcasted_iota(jnp.int32, (tokens, length), 1) <= position
+    scale_factor = 1.0 / math.sqrt(HEAD_DIM)
+
+    def one_head(g, carry):
+        at = pl.ds(pl.multiple_of(g * HEAD_DIM, HEAD_DIM), HEAD_DIM)
+        k, v = kv[0, :, at], kv[1, :, at]
+        for h in range(group):
+            cols = pl.ds(pl.multiple_of(g * group * HEAD_DIM + h * HEAD_DIM, HEAD_DIM), HEAD_DIM)
+            s = lax.dot_general(
+                q_ref[:, cols], k, (((1,), (1,)), ((), ())), preferred_element_type=jnp.float32
+            )
+            s = jnp.where(visible, s * scale_factor, -1e30)
+            w = jnp.where(visible, jnp.exp(s - jnp.max(s, axis=1, keepdims=True)), 0.0)
+            total = jnp.sum(w, axis=1, keepdims=True)
+            mixed = jnp.dot(w.astype(jnp.bfloat16), v, preferred_element_type=jnp.float32)
+            out_ref[:, cols] = (mixed / total).astype(jnp.bfloat16)
+        return carry
+
+    lax.fori_loop(0, k_hbm.shape[1] // HEAD_DIM, one_head, 0)
+    for copy in sent:
+        copy.wait_send()
+
+
+def attend(queries, keys, values, n):
+    rows, width = keys.shape
+    any_spec = pl.BlockSpec(memory_space=pl.ANY)
+    return pl.pallas_call(
+        functools.partial(attend_kernel, n),
+        out_shape=jax.ShapeDtypeStruct(queries.shape, jnp.bfloat16),
+        in_specs=[any_spec] * 3,
+        out_specs=pl.BlockSpec(memory_space=pltpu.VMEM),
+        scratch_shapes=[
+            pltpu.VMEM(queries.shape, jnp.bfloat16),
+            pltpu.VMEM((2, n * rows, width), jnp.bfloat16),
+            pltpu.SemaphoreType.DMA((3,)),
+            pltpu.SemaphoreType.DMA((n // 4,)),
+            pltpu.SemaphoreType.DMA((n // 4,)),
+            pltpu.SemaphoreType.DMA((n // 2,)),
+            pltpu.SemaphoreType.DMA((n,)),
+        ],
+        compiler_params=pltpu.CompilerParams(
+            collective_id=0, has_side_effects=True, vmem_limit_bytes=48 << 20
+        ),
+        name="attend",
+    )(queries, keys, values)
+
+
+def experts_kernel(
+    n, normed, place, mix, order, order_t, w_gate, w_up, w_down, out_ref,
+    gate_w, up_w, down_w, packed, disp, rows_x, gu_send, gu_own, gu_recv, hidden, parts, group_parts,
+    back, returned, w_sem, own_sem, d_send, f_send, d_recv, x_send, x_recv, h_send, h_recv,
+    g_send, g_recv, r_send, r_recv,
+):
+    me, sec = lax.axis_index("ctx"), lax.axis_index("sec")
+    members = n // EXPERTS
+    block = EXPERTS // CHUNKS
+    e, j = me // members, me % members
+    b, el = e // block, e % block
+    width = packed.shape[2]
+    half = gate_w.shape[1] // 2
+    chunk_rows = block * members * CAP
+    tile = 256
+
+    loads = [
+        pltpu.make_async_copy(w_gate, gate_w, w_sem.at[0]),
+        pltpu.make_async_copy(w_up, up_w, w_sem.at[1]),
+        pltpu.make_async_copy(w_down, down_w, w_sem.at[2]),
+    ]
+    for load in loads:
+        load.start()
+
+    def expert_at(q, i, sign):
+        return ((b + CHUNKS + sign * q) % CHUNKS) * block + (el + block + sign * i) % block
+
+    others = [(q, i) for q in range(CHUNKS) for i in range(block) if (q, i) != (0, 0)]
+    barrier = pltpu.get_barrier_semaphore()
+    for q, i in others:
+        pl.semaphore_signal(
+            barrier, inc=1, device_id=on_ctx(expert_at(q, i, 1) * members + j), device_id_type=MESH
+        )
+    for g in range(1, members):
+        pl.semaphore_signal(
+            barrier, inc=1, device_id=on_ctx(e * members + (j + g) % members), device_id_type=MESH
+        )
+    pl.semaphore_signal(barrier, inc=1, device_id={"sec": 1 - sec}, device_id_type=MESH)
+
+    stacked = jnp.concatenate([normed[:, c * width:(c + 1) * width] for c in range(SPLIT)], axis=0)
+    for x in range(EXPERTS):
+        packed[x] = jnp.dot(
+            place[x * UNIT:(x + 1) * UNIT, :], stacked, preferred_element_type=jnp.float32
+        ).astype(jnp.bfloat16)
+    pl.semaphore_wait(barrier, EXPERTS - 1 + members)
+
+    sent = []
+
+    def remote(src, dst, send_sem, recv_sem, device):
+        return pltpu.make_async_remote_copy(
+            src_ref=src, dst_ref=dst, send_sem=send_sem, recv_sem=recv_sem,
+            device_id=device, device_id_type=MESH,
+        )
+
+    def send(src, dst, send_sem, recv_sem, device):
+        copy = remote(src, dst, send_sem, recv_sem, device)
+        copy.start()
+        sent.append(copy)
+
+    def wait_for(dst, recv_sem):
+        remote(dst, dst, d_send.at[0], recv_sem, {"sec": 1 - sec}).wait_recv()
+
+    for number, (q, i) in enumerate(others):
+        target = expert_at(q, i, 1)
+        send(packed.at[target], disp.at[me], d_send.at[number], d_recv.at[me], on_ctx(target * members + j))
+    own = pltpu.make_async_copy(packed.at[e], disp.at[me], own_sem.at[0])
+    own.start()
+    for g in range(1, members):
+        send(
+            packed.at[e], disp.at[me], f_send.at[0, g - 1], d_recv.at[me],
+            on_ctx(e * members + (j + g) % members),
+        )
+
+    def first_slot(q):
+        return ((b + CHUNKS - q) % CHUNKS) * block * members
+
+    def forward(q):
+        for i in range(block):
+            if (q, i) == (0, 0):
+                continue
+            source = expert_at(q, i, -1) * members + j
+            wait_for(disp.at[source], d_recv.at[source])
+            for g in range(1, members):
+                send(
+                    disp.at[source], disp.at[source], f_send.at[q * block + i, g - 1], d_recv.at[source],
+                    on_ctx(e * members + (j + g) % members),
+                )
+
+    def gate_up(q):
+        if q == 0:
+            own.wait()
+        for i in range(block):
+            for g in range(1, members):
+                source = expert_at(q, i, -1) * members + (j + g) % members
+                wait_for(disp.at[source], d_recv.at[source])
+        first = first_slot(q)
+        for u in range(block * members // PAIR):
+            flat = disp[pl.ds(first + u * PAIR, PAIR)].reshape(PAIR * UNIT, width)
+            tall = jnp.dot(order[...], flat, preferred_element_type=jnp.float32).astype(jnp.bfloat16)
+            for c in range(SPLIT):
+                rows_x[u * PAIR * CAP:(u + 1) * PAIR * CAP, c * width:(c + 1) * width] = tall[
+                    c * PAIR * CAP:(c + 1) * PAIR * CAP
+                ]
+        if q == 0:
+            loads[0].wait()
+            loads[1].wait()
+
+        def product(weights, base, t):
+            at = pl.ds(pl.multiple_of(base + t * tile, tile), tile)
+            return jnp.dot(rows_x[...], weights[:, at], preferred_element_type=jnp.float32)
+
+        def peers(t, carry):
+            at = pl.multiple_of(t * tile, tile)
+            gu_send[q, :, pl.ds(at, tile)] = product(gate_w, (1 - sec) * half, t).astype(jnp.bfloat16)
+            gu_send[q, :, pl.ds(at + half, tile)] = product(up_w, (1 - sec) * half, t).astype(jnp.bfloat16)
+            return carry
+
+        def mine(t, carry):
+            at = pl.multiple_of(t * tile, tile)
+            gu_own[q, :, pl.ds(at, tile)] = product(gate_w, sec * half, t)
+            gu_own[q, :, pl.ds(at + half, tile)] = product(up_w, sec * half, t)
+            return carry
+
+        lax.fori_loop(0, half // tile, peers, 0)
+        send(gu_send.at[q], gu_recv.at[q], x_send.at[q], x_recv.at[q], {"sec": 1 - sec})
+        lax.fori_loop(0, half // tile, mine, 0)
+
+    def activate(q):
+        wait_for(gu_recv.at[q], x_recv.at[q])
+        full = gu_own[q] + gu_recv[q].astype(jnp.float32)
+        gate, up = full[:, :half], full[:, half:]
+        hidden[sec, q] = (gate / (1.0 + jnp.exp(-gate)) * up).astype(jnp.bfloat16)
+        send(hidden.at[sec, q], hidden.at[sec, q], h_send.at[q], h_recv.at[q], {"sec": 1 - sec})
+
+    def down(q):
+        wait_for(hidden.at[1 - sec, q], h_recv.at[q])
+        if q == 0:
+            loads[2].wait()
+        first = first_slot(q)
+        both = jnp.concatenate([hidden[0, q], hidden[1, q]], axis=1)
+        wide = [
+            jnp.dot(both, down_w[:, c * width:(c + 1) * width], preferred_element_type=jnp.float32).astype(
+                jnp.bfloat16
+            )
+            for c in range(SPLIT)
+        ]
+        for u in range(block * members // PAIR):
+            tall = jnp.concatenate([w[u * PAIR * CAP:(u + 1) * PAIR * CAP] for w in wide], axis=0)
+            flat = jnp.dot(order_t[...], tall, preferred_element_type=jnp.float32).astype(jnp.bfloat16)
+            for s in range(PAIR):
+                at = first + u * PAIR + s
+                parts[at // members, at % members] = flat[s * UNIT:(s + 1) * UNIT]
+        start = first // members
+        for g in range(1, members):
+            to = (j + g) % members
+            send(
+                parts.at[pl.ds(start, block), to], group_parts.at[g - 1, pl.ds(start, block)],
+                g_send.at[q, g - 1], g_recv.at[q, g - 1], on_ctx(e * members + to),
+            )
+
+    def give_back(q):
+        start = first_slot(q) // members
+        for g in range(1, members):
+            wait_for(group_parts.at[g - 1, pl.ds(start, block)], g_recv.at[q, g - 1])
+        for i in range(block):
+            source = expert_at(q, i, -1)
+            total = parts[source, j].astype(jnp.float32)
+            for g in range(1, members):
+                total = total + group_parts[g - 1, source].astype(jnp.float32)
+            if (q, i) == (0, 0):
+                returned[e] = total.astype(jnp.bfloat16)
+            else:
+                back[source] = total.astype(jnp.bfloat16)
+                send(
+                    back.at[source], returned.at[e], r_send.at[q * block + i], r_recv.at[e],
+                    on_ctx(source * members + j),
+                )
+
+    stages = (forward, gate_up, activate, down, give_back)
+    lag = (0, 0, 1, 1, 2)
+    for step in range(CHUNKS + max(lag)):
+        for stage, delay in sorted(zip(stages, lag), key=lambda pair: pair[1]):
+            if 0 <= step - delay < CHUNKS:
+                stage(step - delay)
+
+    for q, i in others:
+        target = expert_at(q, i, 1)
+        wait_for(returned.at[target], r_recv.at[target])
+    flat = returned[...].reshape(EXPERTS * UNIT, width)
+    tokens = out_ref.shape[0]
+    for c in range(SPLIT):
+        both = jnp.dot(
+            mix[c * 2 * tokens:(c + 1) * 2 * tokens, :], flat, preferred_element_type=jnp.float32
+        )
+        out_ref[:, c * width:(c + 1) * width] = (both[:tokens] + both[tokens:]).astype(jnp.bfloat16)
+    for copy in sent:
+        copy.wait_send()
+
+
+def run_experts(normed, place, mix, w_gate, w_up, w_down, n):
+    tokens, wide = normed.shape
+    width = wide // SPLIT
+    members = n // EXPERTS
+    ff = w_gate.shape[1]
+    chunk_rows = n * CAP // CHUNKS
+    block = EXPERTS // CHUNKS
+    tall = np.arange(PAIR * UNIT)
+    column, rest = tall // (PAIR * CAP), tall % (PAIR * CAP)
+    origin = (rest // CAP) * UNIT + column * CAP + rest % CAP
+    perm = np.zeros((PAIR * UNIT, PAIR * UNIT), np.float32)
+    perm[tall, origin] = 1.0
+    order = jnp.asarray(perm, jnp.bfloat16)
+    order_t = jnp.asarray(perm.T, jnp.bfloat16)
+    vmem = pl.BlockSpec(memory_space=pltpu.VMEM)
+    any_spec = pl.BlockSpec(memory_space=pl.ANY)
+    bf16 = jnp.bfloat16
+    dma = pltpu.SemaphoreType.DMA
+    more = max(members - 1, 1)
+    return pl.pallas_call(
+        functools.partial(experts_kernel, n),
+        out_shape=jax.ShapeDtypeStruct((tokens, wide), bf16),
+        in_specs=[vmem] * 5 + [any_spec] * 3,
+        out_specs=vmem,
+        scratch_shapes=[
+            pltpu.VMEM(w_gate.shape, bf16),
+            pltpu.VMEM(w_up.shape, bf16),
+            pltpu.VMEM(w_down.shape, bf16),
+            pltpu.VMEM((EXPERTS, UNIT, width), bf16),
+            pltpu.VMEM((n, UNIT, width), bf16),
+            pltpu.VMEM((chunk_rows, wide), bf16),
+            pltpu.VMEM((CHUNKS, chunk_rows, ff), bf16),
+            pltpu.VMEM((CHUNKS, chunk_rows, ff), jnp.float32),
+            pltpu.VMEM((CHUNKS, chunk_rows, ff), bf16),
+            pltpu.VMEM((2, CHUNKS, chunk_rows, ff // 2), bf16),
+            pltpu.VMEM((EXPERTS, members, UNIT, width), bf16),
+            pltpu.VMEM((more, EXPERTS, UNIT, width), bf16),
+            pltpu.VMEM((EXPERTS, UNIT, width), bf16),
+            pltpu.VMEM((EXPERTS, UNIT, width), bf16),
+            dma((3,)),
+            dma((1,)),
+            dma((EXPERTS,)),
+            dma((EXPERTS, more)),
+            dma((n,)),
+            dma((CHUNKS,)),
+            dma((CHUNKS,)),
+            dma((CHUNKS,)),
+            dma((CHUNKS,)),
+            dma((CHUNKS, more)),
+            dma((CHUNKS, more)),
+            dma((EXPERTS,)),
+            dma((EXPERTS,)),
+        ],
+        compiler_params=pltpu.CompilerParams(
+            collective_id=1, has_side_effects=True, vmem_limit_bytes=60 << 20
+        ),
+        name="experts",
+    )(normed, place, mix, order, order_t, w_gate, w_up, w_down)
+
+
+def experts_by_kernel(normed, cells, combine, w_gate, w_up, w_down, n):
+    tokens = normed.shape[0]
+    unit = np.arange(EXPERTS * UNIT)
+    cell = jnp.asarray((unit // UNIT) * CAP + unit % CAP, jnp.int32)
+    column = jnp.asarray((unit % UNIT) // CAP, jnp.int32)
+    split = jnp.arange(SPLIT, dtype=jnp.int32)
+    same = column[:, None] == split[None, :]
+    taken = (cells[:, 0][None, :] == cell[:, None]) | (cells[:, 1][None, :] == cell[:, None])
+    place = (same[:, :, None] & taken[:, None, :]).astype(jnp.bfloat16)
+    place = place.reshape(EXPERTS * UNIT, SPLIT * tokens)
+    share = jnp.where(cells[:, 0][:, None] == cell[None, :], combine[:, 0][:, None], 0.0) + jnp.where(
+        cells[:, 1][:, None] == cell[None, :], combine[:, 1][:, None], 0.0
+    )
+    coarse = share.astype(jnp.bfloat16)
+    fine = (share - lax.reduce_precision(share, 8, 7)).astype(jnp.bfloat16)
+    both = jnp.stack([coarse, fine])
+    mix = jnp.where((split[:, None] == column[None, :])[:, None, None, :], both[None], 0)
+    mix = mix.astype(jnp.bfloat16).reshape(SPLIT * 2 * tokens, EXPERTS * UNIT)
+    return run_experts(normed, place, mix, w_gate, w_up, w_down, n)
 
 
 def on_device(queries, keys, values, gain, router, w_gate, w_up, w_down, routes):
     cycle_size = lax.axis_size("ctx")
     token_count = queries.shape[0]
-    kv_rows = keys.shape[0]
-    cache = (kv_rows - token_count) * cycle_size
-    query_pos = (
-        cache + lax.axis_index("ctx") * token_count + jnp.arange(token_count, dtype=jnp.int32)
-    )
-    kv_local = keys.shape[1] // HEAD_DIM
-    group_size = HEADS // KV_HEADS
-    query_heads = queries.reshape(token_count, kv_local, group_size, HEAD_DIM)
-    scale_factor = 1.0 / math.sqrt(HEAD_DIM)
-    pieces = (
-        lax.all_gather(keys, "ctx", axis=0, tiled=True),
-        lax.all_gather(values, "ctx", axis=0, tiled=True),
-    )
-    running = jnp.full((kv_local, group_size, token_count), -1e30, jnp.float32)
-    key_piece = pieces[0].reshape(pieces[0].shape[0], kv_local, HEAD_DIM)
-    value_piece = pieces[1].reshape(pieces[1].shape[0], kv_local, HEAD_DIM)
-    key_pos = jnp.arange(key_piece.shape[0], dtype=jnp.int32)
-    visible = key_pos[None, :] <= query_pos[:, None]
-    scores = (
-        jnp.einsum("tgqd,ngd->gqtn", query_heads, key_piece, preferred_element_type=jnp.float32)
-        * scale_factor
-    )
-    scores = jnp.where(visible, scores, -1e30)
-    newest = jnp.maximum(running, jnp.max(scores, axis=3))
-    weights = jnp.where(visible, jnp.exp(scores - newest[..., None]), 0.0)
-    total = jnp.sum(weights, axis=3)
-    mixed = jnp.einsum(
-        "gqtn,ngd->gqtd",
-        weights.astype(jnp.bfloat16),
-        value_piece,
-        preferred_element_type=jnp.float32,
-    )
-    accum = mixed
-    running, total, accum = (newest, total, accum)
-    attended = (
-        (accum / total[..., None])
-        .transpose(2, 0, 1, 3)
-        .reshape(token_count, kv_local * group_size * HEAD_DIM)
-    )
-    attended = attended.astype(jnp.bfloat16)
+    attended = attend(queries, keys, values, cycle_size)
     attn_float = attended.astype(jnp.float32)
     gained = attn_float * gain[None, :]
     part_squares = jnp.sum(attn_float * attn_float, axis=1)
@@ -74,6 +442,11 @@
     before = jnp.cumsum(hot, axis=0) - hot
     slots = jnp.sum(before * hot, axis=1)
     cells = flat_routes * CAP + slots
+    if cycle_size * CAP <= 640:
+        moe_out = experts_by_kernel(
+            normed, cells.reshape(token_count, TOP), combine, w_gate, w_up, w_down, cycle_size
+        )
+        return (normed, moe_out)
     placing = (cells[:, None] == jnp.arange(EXPERTS * CAP, dtype=jnp.int32)[None, :]).astype(
         jnp.float32
     )

time: 303 us -> 137 us (0.45)
  waiting for transfers between devices: 121 us -> 0 us
  blocking collectives: 123 us -> 3.84 us
  Pallas kernels: 0 us -> 116 us
  matrix products: 26.8 us -> 1.43 us
  between operations: 14 us -> 0.74 us
  local copies, waits for them, and re-layouts: 11.5 us -> 6.57 us
  other arithmetic: 4.43 us -> 7.64 us
    all_to_all x2 -> x0, blocking collectives: 119 us -> none  [the longest x1 59.8 us: on_device(): lax.all_to_all(down_part, 'ctx', split_axis=0, concat_axis=0, tiled=True)]
    pallas_call x0 -> x2, Pallas kernels: none -> 116 us  [the longest x1 80.9 us: run_experts(): pl.pallas_call(functools.partial(experts_kernel, n), out_shape=jax.ShapeD...]
    all_gather x2 -> x0, waiting for transfers between devices: 68.5 us -> none  [the longest x1 37.2 us: on_device(): lax.all_gather(keys, 'ctx', axis=0, tiled=True)]
    psum x1 -> x0, waiting for transfers between devices: 50.7 us -> none  [on_device(): up_full = lax.psum(up_part.astype(jnp.bfloat16), 'sec').astype(jnp.float32)]
    dot_general x7 -> x0, matrix products: 26.1 us -> none  [the longest x1 6.47 us: on_device(): jnp.einsum('sid,df->sif', received, w_gate, preferred_element_type=jnp.fl...]
    all_gather x2 -> x0, local copies, waits for them, and re-layouts: 3.19 us -> none  [the longest x1 1.6 us: on_device(): lax.all_gather(keys, 'ctx', axis=0, tiled=True)]
  transfers between devices with their start and end apart: 3 -> 0, of which waited for: 3 -> 0; matrix products, arithmetic and copies ran while one was open for 3% -> 0% of each run, Pallas kernels for 0% -> 0%
where the time goes in v1:
time: 137 us
  Pallas kernels  116 us (85%)
  other arithmetic  7.64 us (6%)
  local copies, waits for them, and re-layouts  6.57 us (5%)
  blocking collectives  3.84 us (3%)
  matrix products  1.43 us (1%)
    pallas_call x1, Pallas kernels, run_experts(): pl.pallas_call(functools.partial(experts_kernel, n), out_shape=jax.ShapeD...  80.9 us
    pallas_call x1, Pallas kernels, attend(): pl.pallas_call(functools.partial(attend_kernel, n), out_shape=jax.ShapeDt...  35.4 us
    unnamed x10, local copies, waits for them, and re-layouts  5.31 us
    psum x1, blocking collectives, on_device(): squares, logits = lax.psum((part_squares, part_logits), 'sec')  3.84 us

profile of v1, /device:TPU:9, one launch (start us, length us, event | category | flops | bytes accessed | tf_op | source)
XLA Modules:
  0.0 136.5 jit_solution(11852061300663861132)
XLA Ops:
  0.6 0.0 copy-start
  0.6 0.7 iota_compare_fusion.1
  1.4 0.7 iota_compare_fusion.2
  2.1 0.8 copy.30
  2.8 0.1 eq.147
  3.0 0.1 fusion.7
  3.1 0.2 reduce_window_sum.11
  3.2 0.2 select_reduce_fusion
  3.4 0.1 reduce_sum.40
  3.6 0.1 copy.31
  3.6 0.7 multiply_add_fusion
  4.3 0.8 compare_or_fusion
  5.1 0.1 and_convert_fusion
  5.2 0.9 copy.32.place
  6.1 0.0 copy-start.1
  6.1 1.0 copy-done.1
  7.1 0.0 copy-start.2
  7.1 0.9 copy-done.2
  8.0 0.0 copy-start.3
  8.0 0.9 copy-done.3
  8.9 35.4 %attend.1 = bf16[64,3072]{1,0:T(8,128)(2,1)S(1)} custom-call(bf16[64,3072]{1,0:T(8,128)(2,1)S(1)} %copy-done.1, bf16[80,512]{1,0:T(8,128)(2,1)S(1)} %copy-done.2, bf16[80,512]{1,0:T(8,128)(2,1)S(1)} %copy-done.3), custom_call_target="tpu_custom_call" | custom-call | tf_op jit(solution)/shard_map/attend/pallas_call | solution.py:123
  44.3 0.2 fusion.3
  44.5 0.0 copy-done
  44.5 1.4 %fusion = f32[64,8]{0,1:T(8,128)S(1)} fusion(f32[3072,8]{0,1:T(8,128)S(1)} %copy-done, bf16[64,3072]{1,0:T(8,128)(2,1)S(1)} %attend.1, f32[3072]{0:T(1024)} %param.16), kind=kOutput, calls=%fused_computation.2 | convolution fusion | flops 19267584 | bytes 505856 | tf_op jit(solution)/shard_map/dot_general | solution.py:431
  45.9 3.8 %all-reduce = (f32[64]{0:T(128)S(1)}, f32[64,8]{0,1:T(8,128)S(1)}) all-reduce(f32[64]{0:T(128)S(1)} %fusion.3, f32[64,8]{0,1:T(8,128)S(1)} %fusion), channel_id=1, replica_groups=mesh['ctx'=16,'sec'=2] {'sec'}, use_global_device_ids=true, to_apply=%region_1.0 | all-reduce | flops 576 | bytes 4608 | tf_op jit(solution)/shard_map/psum | solution.py:432
  49.8 1.6 %fusion.2.normed = bf16[64,3072]{1,0:T(8,128)(2,1)} fusion(bf16[64,3072]{1,0:T(8,128)(2,1)S(1)} %attend.1, f32[64]{0:T(128)S(1)} %add_rsqrt_fusion, f32[3072]{0:T(1024)} %param.16), kind=kLoop, calls=%fused_computation.4 | loop fusion | flops 786432 | bytes 798976 | tf_op jit(solution)/shard_map/convert_element_type | solution.py:434
  51.3 0.7 select_reduce_fusion.1
  52.1 0.8 fusion.6
  52.9 0.9 broadcast_select_fusion
  53.9 80.9 %experts.1 = bf16[64,3072]{1,0:T(8,128)(2,1)} custom-call(bf16[64,3072]{1,0:T(8,128)(2,1)} %fusion.2.normed, bf16[640,256]{1,0:T(8,128)(2,1)} %copy.32.place, bf16[512,640]{1,0:T(8,128)(2,1)} %bitcast.11, bf16[320,320]{1,0:T(8,128)(2,1)} %constant.28.clone.order.order_t, bf16[320,320]{1,0:T(8,128)(2,1)} %constant.28.clone.order.order_t, ...), custom_call_target="tpu_custom_call" | custom-call | tf_op jit(solution)/shard_map/experts/pallas_call | solution.py:362
  134.7 1.8 %copy.34 = bf16[64,3072]{1,0:T(8,128)(2,1)} copy(bf16[64,3072]{1,0:T(8,128)(2,1)} %experts.1) | data formatting | bytes 786432
  (7 shorter events, 0.1 us)
Async XLA Ops:
  0.6 43.9 %copy-start = (f32[3072,8]{0,1:T(8,128)S(1)}, f32[3072,8]{0,1:T(8,128)}, u32[]{:S(2)}) copy-start(f32[3072,8]{0,1:T(8,128)} %param.17) | copy-start | bytes 294916
  6.1 1.0 copy-start.1
  7.1 0.9 copy-start.2
  8.0 0.9 copy-start.3

commit v2 on v1

--- a/solution.py
+++ b/solution.py
@@ -18,7 +18,7 @@
 CAP = 20
 SPLIT = 4
 UNIT = CAP * SPLIT
-CHUNKS = 2
+CHUNKS = 4
 PAIR = 4
 MESH = pl.DeviceIdType.MESH
 
@@ -27,8 +27,11 @@
     return {"ctx": index}
 
 
-def attend_kernel(n, q_hbm, k_hbm, v_hbm, out_ref, q_ref, kv, local_sem, z_send, y_send, c_send, recv):
-    me = lax.axis_index("ctx")
+def attend_kernel(
+    n, q_hbm, k_hbm, v_hbm, gain, router, normed, logits, q_ref, kv, q_rows, top, total, mixed, attended,
+    stats, stats_in, local_sem, z_send, y_send, c_send, recv, s_send, s_recv,
+):
+    me, sec = lax.axis_index("ctx"), lax.axis_index("sec")
     far = n // 4
     zi, yi, ci = me // 4, (me // 2) % 2, me % 2
     rows = k_hbm.shape[0]
@@ -53,7 +56,8 @@
         )
     for peer in (y_peer, c_peer):
         pl.semaphore_signal(barrier, inc=1, device_id=on_ctx(peer), device_id_type=MESH)
-    pl.semaphore_wait(barrier, far + 1)
+    pl.semaphore_signal(barrier, inc=1, device_id={"sec": 1 - sec}, device_id_type=MESH)
+    pl.semaphore_wait(barrier, far + 2)
     loads[0].wait()
     loads[1].wait()
     sent = []
@@ -72,78 +76,146 @@
             device_id=on_ctx(c_peer), device_id_type=MESH,
         ).wait_recv()
 
+    tokens, wide = q_ref.shape
+    group = HEADS // KV_HEADS
+    heads = k_hbm.shape[1] // HEAD_DIM
+    length = 4 * rows
+    position = (rows - tokens) * n + me * tokens + lax.broadcasted_iota(jnp.int32, (tokens, length), 0)
+    lane = lax.broadcasted_iota(jnp.int32, (tokens, length), 1)
+    scale_factor = 1.0 / math.sqrt(HEAD_DIM)
+
+    def attend_to(k):
+        z = (zi + far - k) % far
+        visible = (lane + z * length <= position)[None]
+        span = pl.ds(pl.multiple_of(z * length, 16), length)
+
+        def one_head(g, carry):
+            at = pl.ds(pl.multiple_of(g * HEAD_DIM, HEAD_DIM), HEAD_DIM)
+            scores = lax.dot_general(
+                q_rows[g], kv[0, span, at], (((1,), (1,)), ((), ())), preferred_element_type=jnp.float32
+            )
+            scores = scores.reshape(group, tokens, length) * scale_factor
+            scores = jnp.where(visible, scores, -1e30).reshape(group * tokens, length)
+            newest = jnp.max(scores, axis=1, keepdims=True)
+            if k > 0:
+                newest = jnp.maximum(newest, top[g])
+            w = jnp.exp(scores - newest)
+            add = jnp.sum(w, axis=1, keepdims=True)
+            out = jnp.dot(w.astype(jnp.bfloat16), kv[1, span, at], preferred_element_type=jnp.float32)
+            if k > 0:
+                fade = jnp.exp(top[g] - newest)
+                add = add + fade * total[g]
+                out = out + fade * mixed[g]
+            top[g] = newest
+            total[g] = add
+            mixed[g] = out
+            return carry
+
+        lax.fori_loop(0, heads, one_head, 0)
+
+    def z_forward(k):
+        source = ((zi + far - k) % far) * 4 + yi * 2 + ci
+        arrived(source)
+        send(source, y_peer, y_send.at[k])
+        send(source, c_peer, c_send.at[k])
+
+    def y_forward(k):
+        source = ((zi + far - k) % far) * 4 + (1 - yi) * 2 + ci
+        arrived(source)
+        send(source, c_peer, c_send.at[far + k])
+
+    def c_wait(k):
+        for y in range(2):
+            arrived(((zi + far - k) % far) * 4 + y * 2 + 1 - ci)
+
     for k in range(1, far):
         send(me, ((zi + k) % far) * 4 + yi * 2 + ci, z_send.at[k - 1])
     send(me, y_peer, y_send.at[0])
     send(me, c_peer, c_send.at[0])
+    loads[2].wait()
+    for g in range(heads):
+        for h in range(group):
+            column = (g * group + h) * HEAD_DIM
+            q_rows[g, h * tokens:(h + 1) * tokens, :] = q_ref[:, column:column + HEAD_DIM]
+    y_forward(0)
+    c_wait(0)
     for k in range(1, far):
-        source = ((zi + far - k) % far) * 4 + yi * 2 + ci
-        arrived(source)
-        send(source, y_peer, y_send.at[k])
-        send(source, c_peer, c_send.at[k])
-    for k in range(far):
-        source = ((zi + far - k) % far) * 4 + (1 - yi) * 2 + ci
-        arrived(source)
-        send(source, c_peer, c_send.at[far + k])
-    for k in range(far):
-        for y in range(2):
-            arrived(((zi + far - k) % far) * 4 + y * 2 + 1 - ci)
-    loads[2].wait()
-
-    tokens = q_ref.shape[0]
-    group = HEADS // KV_HEADS
-    length = n * rows
-    position = (rows - tokens) * n + me * tokens + lax.broadcasted_iota(jnp.int32, (tokens, length), 0)
-    visible = lax.broadcasted_iota(jnp.int32, (tokens, length), 1) <= position
-    scale_factor = 1.0 / math.sqrt(HEAD_DIM)
-
-    def one_head(g, carry):
-        at = pl.ds(pl.multiple_of(g * HEAD_DIM, HEAD_DIM), HEAD_DIM)
-        k, v = kv[0, :, at], kv[1, :, at]
+        z_forward(k)
+        attend_to(k - 1)
+        y_forward(k)
+        c_wait(k)
+    attend_to(far - 1)
+
+    squares = jnp.zeros((tokens, 1), jnp.float32)
+    for g in range(heads):
         for h in range(group):
-            cols = pl.ds(pl.multiple_of(g * group * HEAD_DIM + h * HEAD_DIM, HEAD_DIM), HEAD_DIM)
-            s = lax.dot_general(
-                q_ref[:, cols], k, (((1,), (1,)), ((), ())), preferred_element_type=jnp.float32
-            )
-            s = jnp.where(visible, s * scale_factor, -1e30)
-            w = jnp.where(visible, jnp.exp(s - jnp.max(s, axis=1, keepdims=True)), 0.0)
-            total = jnp.sum(w, axis=1, keepdims=True)
-            mixed = jnp.dot(w.astype(jnp.bfloat16), v, preferred_element_type=jnp.float32)
-            out_ref[:, cols] = (mixed / total).astype(jnp.bfloat16)
-        return carry
-
-    lax.fori_loop(0, k_hbm.shape[1] // HEAD_DIM, one_head, 0)
+            column = (g * group + h) * HEAD_DIM
+            part = slice(h * tokens, (h + 1) * tokens)
+            out = (mixed[g, part, :] / total[g, part, :]).astype(jnp.bfloat16).astype(jnp.float32)
+            squares = squares + jnp.sum(out * out, axis=1, keepdims=True)
+            attended[:, column:column + HEAD_DIM] = out * gain[:, column:column + HEAD_DIM]
+    stats[0] = jnp.zeros_like(stats[0])
+    stats[0, :, :EXPERTS] = jnp.dot(
+        attended[...], router[...], preferred_element_type=jnp.float32, precision=lax.Precision.HIGHEST
+    )
+    stats[1] = jnp.broadcast_to(squares, stats.shape[1:])
+    swap = pltpu.make_async_remote_copy(
+        src_ref=stats, dst_ref=stats_in, send_sem=s_send.at[0], recv_sem=s_recv.at[0],
+        device_id={"sec": 1 - sec}, device_id_type=MESH,
+    )
+    swap.start()
+    swap.wait()
+    factor = lax.rsqrt((stats[1] + stats_in[1]) / D + 1e-05)
+    logits[...] = (stats[0] + stats_in[0]) * factor
+    normed[...] = (attended[...] * factor[:, :1]).astype(jnp.bfloat16)
     for copy in sent:
         copy.wait_send()
 
 
-def attend(queries, keys, values, n):
+def attend(queries, keys, values, gain, router, n):
     rows, width = keys.shape
-    any_spec = pl.BlockSpec(memory_space=pl.ANY)
+    tokens = queries.shape[0]
+    group = HEADS // KV_HEADS
+    heads = width // HEAD_DIM
+    hbm = pl.BlockSpec(memory_space=pltpu.HBM)
+    vmem = pl.BlockSpec(memory_space=pltpu.VMEM)
+    f32 = jnp.float32
     return pl.pallas_call(
         functools.partial(attend_kernel, n),
-        out_shape=jax.ShapeDtypeStruct(queries.shape, jnp.bfloat16),
-        in_specs=[any_spec] * 3,
-        out_specs=pl.BlockSpec(memory_space=pltpu.VMEM),
+        out_shape=(
+            jax.ShapeDtypeStruct(queries.shape, jnp.bfloat16),
+            jax.ShapeDtypeStruct((tokens, 128), f32),
+        ),
+        in_specs=[hbm] * 3 + [vmem] * 2,
+        out_specs=(vmem, vmem),
         scratch_shapes=[
             pltpu.VMEM(queries.shape, jnp.bfloat16),
             pltpu.VMEM((2, n * rows, width), jnp.bfloat16),
+            pltpu.VMEM((heads, group * tokens, HEAD_DIM), jnp.bfloat16),
+            pltpu.VMEM((heads, group * tokens, 1), f32),
+            pltpu.VMEM((heads, group * tokens, 1), f32),
+            pltpu.VMEM((heads, group * tokens, HEAD_DIM), f32),
+            pltpu.VMEM(queries.shape, f32),
+            pltpu.VMEM((2, tokens, 128), f32),
+            pltpu.VMEM((2, tokens, 128), f32),
             pltpu.SemaphoreType.DMA((3,)),
             pltpu.SemaphoreType.DMA((n // 4,)),
             pltpu.SemaphoreType.DMA((n // 4,)),
             pltpu.SemaphoreType.DMA((n // 2,)),
             pltpu.SemaphoreType.DMA((n,)),
+            pltpu.SemaphoreType.DMA((1,)),
+            pltpu.SemaphoreType.DMA((1,)),
         ],
         compiler_params=pltpu.CompilerParams(
             collective_id=0, has_side_effects=True, vmem_limit_bytes=48 << 20
         ),
         name="attend",
-    )(queries, keys, values)
+    )(queries, keys, values, gain.reshape(1, -1), router)
 
 
 def experts_kernel(
-    n, normed, place, mix, order, order_t, w_gate, w_up, w_down, out_ref,
-    gate_w, up_w, down_w, packed, disp, rows_x, gu_send, gu_own, gu_recv, hidden, parts, group_parts,
+    n, normed, logits, routes, order, order_t, w_gate, w_up, w_down, out_ref,
+    mix, gate_w, up_w, down_w, packed, disp, rows_x, gu_send, gu_own, gu_recv, hidden, parts, group_parts,
     back, returned, w_sem, own_sem, d_send, f_send, d_recv, x_send, x_recv, h_send, h_recv,
     g_send, g_recv, r_send, r_recv,
 ):
@@ -165,10 +237,15 @@
     for load in loads:
         load.start()
 
+    def block_at(q):
+        pair = (b // 2 + 1) % 2 if q < 2 else b // 2
+        return pair * 2 + (b % 2 if q % 2 == (0 if q < 2 else 1) else 1 - b % 2)
+
     def expert_at(q, i, sign):
-        return ((b + CHUNKS + sign * q) % CHUNKS) * block + (el + block + sign * i) % block
-
-    others = [(q, i) for q in range(CHUNKS) for i in range(block) if (q, i) != (0, 0)]
+        return block_at(q) * block + (el + block + sign * i) % block
+
+    last = (CHUNKS - 1, 0)
+    others = [(q, i) for q in range(CHUNKS) for i in range(block) if (q, i) != last]
     barrier = pltpu.get_barrier_semaphore()
     for q, i in others:
         pl.semaphore_signal(
@@ -180,11 +257,42 @@
         )
     pl.semaphore_signal(barrier, inc=1, device_id={"sec": 1 - sec}, device_id_type=MESH)
 
+    tokens = normed.shape[0]
+    f32 = jnp.float32
+    lane = lax.broadcasted_iota(jnp.int32, (tokens, 128), 1)
+    picks = [(lane == routes[:, k:k + 1]).astype(f32) for k in range(TOP)]
+    earlier = (
+        lax.broadcasted_iota(jnp.int32, (tokens, tokens), 1) < lax.broadcasted_iota(jnp.int32, (tokens, tokens), 0)
+    )
+    before = jnp.dot(
+        earlier.astype(jnp.bfloat16), (picks[0] + picks[1]).astype(jnp.bfloat16), preferred_element_type=f32
+    )
+    chosen = [jnp.sum(pick * logits[...], axis=1, keepdims=True) for pick in picks]
+    cells = [
+        routes[:, k:k + 1].astype(f32) * CAP + jnp.sum(picks[k] * before, axis=1, keepdims=True)
+        for k in range(TOP)
+    ]
+    combine = [1.0 / (1.0 + jnp.exp(chosen[1 - k] - chosen[k])) for k in range(TOP)]
+    spot = lax.broadcasted_iota(jnp.int32, (tokens, EXPERTS * UNIT), 1)
+    unit = (spot * 820) >> 16
+    rest = spot - unit * UNIT
+    column = (rest * 3277) >> 16
+    cell = (unit * CAP + rest - column * CAP).astype(f32)
+    hits = [cell == cells[k] for k in range(TOP)]
+    placing = jnp.where(hits[0] | hits[1], 1.0, 0.0)
+    share = jnp.where(hits[0], combine[0], 0.0) + jnp.where(hits[1], combine[1], 0.0)
+    coarse = share.astype(jnp.bfloat16).astype(f32)
+    fine = share - coarse
+    place = jnp.concatenate([jnp.where(column == c, placing, 0.0) for c in range(SPLIT)], axis=0)
+    for c in range(SPLIT):
+        mix[2 * c * tokens:(2 * c + 1) * tokens, :] = jnp.where(column == c, coarse, 0.0).astype(jnp.bfloat16)
+        mix[(2 * c + 1) * tokens:(2 * c + 2) * tokens, :] = jnp.where(column == c, fine, 0.0).astype(jnp.bfloat16)
     stacked = jnp.concatenate([normed[:, c * width:(c + 1) * width] for c in range(SPLIT)], axis=0)
+    rows_out = lax.dot_general(
+        place.astype(jnp.bfloat16), stacked, (((0,), (0,)), ((), ())), preferred_element_type=f32
+    ).astype(jnp.bfloat16)
     for x in range(EXPERTS):
-        packed[x] = jnp.dot(
-            place[x * UNIT:(x + 1) * UNIT, :], stacked, preferred_element_type=jnp.float32
-        ).astype(jnp.bfloat16)
+        packed[x] = rows_out[x * UNIT:(x + 1) * UNIT]
     pl.semaphore_wait(barrier, EXPERTS - 1 + members)
 
     sent = []
@@ -215,11 +323,11 @@
         )
 
     def first_slot(q):
-        return ((b + CHUNKS - q) % CHUNKS) * block * members
+        return block_at(q) * block * members
 
     def forward(q):
         for i in range(block):
-            if (q, i) == (0, 0):
+            if (q, i) == last:
                 continue
             source = expert_at(q, i, -1) * members + j
             wait_for(disp.at[source], d_recv.at[source])
@@ -230,7 +338,7 @@
                 )
 
     def gate_up(q):
-        if q == 0:
+        if q == CHUNKS - 1:
             own.wait()
         for i in range(block):
             for g in range(1, members):
@@ -310,7 +418,7 @@
             total = parts[source, j].astype(jnp.float32)
             for g in range(1, members):
                 total = total + group_parts[g - 1, source].astype(jnp.float32)
-            if (q, i) == (0, 0):
+            if (q, i) == last:
                 returned[e] = total.astype(jnp.bfloat16)
             else:
                 back[source] = total.astype(jnp.bfloat16)
@@ -330,7 +438,6 @@
         target = expert_at(q, i, 1)
         wait_for(returned.at[target], r_recv.at[target])
     flat = returned[...].reshape(EXPERTS * UNIT, width)
-    tokens = out_ref.shape[0]
     for c in range(SPLIT):
         both = jnp.dot(
             mix[c * 2 * tokens:(c + 1) * 2 * tokens, :], flat, preferred_element_type=jnp.float32
@@ -340,7 +447,7 @@
         copy.wait_send()
 
 
-def run_experts(normed, place, mix, w_gate, w_up, w_down, n):
+def run_experts(normed, logits, routes, w_gate, w_up, w_down, n):
     tokens, wide = normed.shape
     width = wide // SPLIT
     members = n // EXPERTS
@@ -355,7 +462,7 @@
     order = jnp.asarray(perm, jnp.bfloat16)
     order_t = jnp.asarray(perm.T, jnp.bfloat16)
     vmem = pl.BlockSpec(memory_space=pltpu.VMEM)
-    any_spec = pl.BlockSpec(memory_space=pl.ANY)
+    any_spec = pl.BlockSpec(memory_space=pltpu.HBM)
     bf16 = jnp.bfloat16
     dma = pltpu.SemaphoreType.DMA
     more = max(members - 1, 1)
@@ -365,6 +472,7 @@
         in_specs=[vmem] * 5 + [any_spec] * 3,
         out_specs=vmem,
         scratch_shapes=[
+            pltpu.VMEM((SPLIT * 2 * tokens, EXPERTS * UNIT), bf16),
             pltpu.VMEM(w_gate.shape, bf16),
             pltpu.VMEM(w_up.shape, bf16),
             pltpu.VMEM(w_down.shape, bf16),
@@ -397,42 +505,16 @@
             collective_id=1, has_side_effects=True, vmem_limit_bytes=60 << 20
         ),
         name="experts",
-    )(normed, place, mix, order, order_t, w_gate, w_up, w_down)
-
-
-def experts_by_kernel(normed, cells, combine, w_gate, w_up, w_down, n):
-    tokens = normed.shape[0]
-    unit = np.arange(EXPERTS * UNIT)
-    cell = jnp.asarray((unit // UNIT) * CAP + unit % CAP, jnp.int32)
-    column = jnp.asarray((unit % UNIT) // CAP, jnp.int32)
-    split = jnp.arange(SPLIT, dtype=jnp.int32)
-    same = column[:, None] == split[None, :]
-    taken = (cells[:, 0][None, :] == cell[:, None]) | (cells[:, 1][None, :] == cell[:, None])
-    place = (same[:, :, None] & taken[:, None, :]).astype(jnp.bfloat16)
-    place = place.reshape(EXPERTS * UNIT, SPLIT * tokens)
-    share = jnp.where(cells[:, 0][:, None] == cell[None, :], combine[:, 0][:, None], 0.0) + jnp.where(
-        cells[:, 1][:, None] == cell[None, :], combine[:, 1][:, None], 0.0
-    )
-    coarse = share.astype(jnp.bfloat16)
-    fine = (share - lax.reduce_precision(share, 8, 7)).astype(jnp.bfloat16)
-    both = jnp.stack([coarse, fine])
-    mix = jnp.where((split[:, None] == column[None, :])[:, None, None, :], both[None], 0)
-    mix = mix.astype(jnp.bfloat16).reshape(SPLIT * 2 * tokens, EXPERTS * UNIT)
-    return run_experts(normed, place, mix, w_gate, w_up, w_down, n)
+    )(normed, logits, routes, order, order_t, w_gate, w_up, w_down)
 
 
 def on_device(queries, keys, values, gain, router, w_gate, w_up, w_down, routes):
     cycle_size = lax.axis_size("ctx")
     token_count = queries.shape[0]
-    attended = attend(queries, keys, values, cycle_size)
-    attn_float = attended.astype(jnp.float32)
-    gained = attn_float * gain[None, :]
-    part_squares = jnp.sum(attn_float * attn_float, axis=1)
-    part_logits = jnp.dot(gained, router, precision=lax.Precision.HIGHEST)
-    squares, logits = lax.psum((part_squares, part_logits), "sec")
-    factor = lax.rsqrt(squares / D + 1e-05)
-    normed = (gained * factor[:, None]).astype(jnp.bfloat16)
-    logits = logits * factor[:, None]
+    normed, logits = attend(queries, keys, values, gain, router, cycle_size)
+    if cycle_size * CAP <= 640:
+        return (normed, run_experts(normed, logits, routes, w_gate, w_up, w_down, cycle_size))
+    logits = logits[:, :EXPERTS]
     expert_ids = jnp.arange(EXPERTS, dtype=jnp.int32)
     picks = (routes[:, :, None] == expert_ids[None, None, :]).astype(jnp.float32)
     chosen = jnp.sum(picks * logits[:, None, :], axis=2)
@@ -442,11 +524,6 @@
     before = jnp.cumsum(hot, axis=0) - hot
     slots = jnp.sum(before * hot, axis=1)
     cells = flat_routes * CAP + slots
-    if cycle_size * CAP <= 640:
-        moe_out = experts_by_kernel(
-            normed, cells.reshape(token_count, TOP), combine, w_gate, w_up, w_down, cycle_size
-        )
-        return (normed, moe_out)
     placing = (cells[:, None] == jnp.arange(EXPERTS * CAP, dtype=jnp.int32)[None, :]).astype(
         jnp.float32
     )

time: 137 us -> 134 us (0.978)
  other arithmetic: 7.64 us -> 0 us
  Pallas kernels: 116 us -> 123 us
  blocking collectives: 3.84 us -> 0 us
  local copies, waits for them, and re-layouts: 6.57 us -> 10.1 us
  matrix products: 1.43 us -> 0 us
    unnamed x10 -> x18, local copies, waits for them, and re-layouts: 5.31 us -> 10.1 us
    psum x1 -> x0, blocking collectives: 3.84 us -> none  [on_device(): squares, logits = lax.psum((part_squares, part_logits), 'sec')]
    pallas_call x1, Pallas kernels: 80.9 us -> 84.7 us  [run_experts(): pl.pallas_call(functools.partial(experts_kernel, n), out_shape=jax.ShapeD...]
    pallas_call x1, Pallas kernels: 35.4 us -> 38.1 us  [attend(): pl.pallas_call(functools.partial(attend_kernel, n), out_shape=(jax.ShapeD...]
    convert_element_type x4 -> x0, other arithmetic: 2.54 us -> none  [the longest x1 1.57 us: on_device(): normed = (gained * factor[:, None]).astype(jnp.bfloat16)]
    dot_general x1 -> x0, matrix products: 1.43 us -> none  [on_device(): part_logits = jnp.dot(gained, router, precision=lax.Precision.HIGHEST)]
    eq x2 -> x0, other arithmetic: 1.42 us -> none  [the longest x1 0.73 us: experts_by_kernel(): split[:, None] == column[None, :]]
where the time goes in v2:
time: 134 us
  Pallas kernels  123 us (92%)
  local copies, waits for them, and re-layouts  10.1 us (8%)
    pallas_call x1, Pallas kernels, run_experts(): pl.pallas_call(functools.partial(experts_kernel, n), out_shape=jax.ShapeD...  84.7 us
    pallas_call x1, Pallas kernels, attend(): pl.pallas_call(functools.partial(attend_kernel, n), out_shape=(jax.ShapeD...  38.1 us
    unnamed x18, local copies, waits for them, and re-layouts  10.1 us

profile of v2, /device:TPU:9, one launch (start us, length us, event | category | flops | bytes accessed | tf_op | source)
XLA Modules:
  0.0 133.5 jit_solution(9097115565404851161)
XLA Ops:
  0.6 1.4 %copy.13.router = f32[3072,8]{1,0:T(8,128)S(1)} copy(f32[3072,8]{0,1:T(8,128)} %param.15) | data formatting | bytes 196608 | tf_op args[4]
  2.0 0.0 copy-start.2
  2.0 1.0 copy-done.2
  3.0 0.0 copy-start.3
  3.0 0.9 copy-done.3
  3.9 0.0 copy-start.4
  3.9 0.9 copy-done.4
  4.8 0.0 copy-start.6
  4.8 0.7 copy-done.6
  5.5 38.1 %attend.1 = (bf16[64,3072]{1,0:T(8,128)(2,1)S(1)}, f32[64,128]{1,0:T(8,128)S(1)}) custom-call(bf16[64,3072]{1,0:T(8,128)(2,1)S(1)} %copy-done.2, bf16[80,512]{1,0:T(8,128)(2,1)S(1)} %copy-done.3, bf16[80,512]{1,0:T(8,128)(2,1)S(1)} %copy-done.4, f32[1,3072]{1,0:T(1,128)S(1)} %bitcast.1, f32[3072,8]{1,0:T(8,128)S(1)} %copy.13.router), custom_call_target="tpu_custom_call" | custom-call | tf_op jit(solution)/shard_map/attend/pallas_call | solution.py:183
  43.6 0.0 copy-start
  43.6 0.7 copy-done
  44.3 0.0 copy-start.5
  44.3 0.6 copy-done.5
  44.9 1.4 %copy.14.routes = s32[64,2]{1,0:T(8,128)} copy(s32[64,2]{0,1:T(2,128)} %param.19) | data formatting | bytes 1024 | tf_op args[8]
  46.3 0.0 copy-start.1
  46.3 84.7 %experts.1 = bf16[64,3072]{1,0:T(8,128)(2,1)} custom-call(bf16[64,3072]{1,0:T(8,128)(2,1)} %copy-done, f32[64,128]{1,0:T(8,128)} %copy-done.5, s32[64,2]{1,0:T(8,128)} %copy.14.routes, bf16[320,320]{1,0:T(8,128)(2,1)} %constant.2.clone.order.order_t, bf16[320,320]{1,0:T(8,128)(2,1)} %constant.2.clone.order.order_t, bf16[3072,1024]{1,0:T(8,128)(2,1)} %w_gate.1, ...), custom_call_target="tpu_custom_call" | custom-call | tf_op jit(solution)/shard_map/experts/pallas_call | solution.py:469
  131.0 0.0 copy-done.1
  131.0 0.7 copy.17
  131.7 1.8 %copy.18 = bf16[64,3072]{1,0:T(8,128)(2,1)} copy(bf16[64,3072]{1,0:T(8,128)(2,1)} %experts.1) | data formatting | bytes 786432
Async XLA Ops:
  2.0 1.0 copy-start.2
  3.0 0.9 copy-start.3
  3.9 0.9 copy-start.4
  4.8 0.7 copy-start.6
  43.6 0.7 copy-start
  44.3 0.6 copy-start.5
  46.3 84.7 %copy-start.1 = (bf16[64,3072]{1,0:T(8,128)(2,1)S(1)}, bf16[64,3072]{1,0:T(8,128)(2,1)}, u32[]{:S(2)}) copy-start(bf16[64,3072]{1,0:T(8,128)(2,1)} %copy-done) | copy-start | bytes 1179652

commit v3 on v2

--- a/solution.py
+++ b/solution.py
@@ -3,7 +3,6 @@
 
 import jax
 import jax.numpy as jnp
-import numpy as np
 from jax import lax
 from jax.experimental import pallas as pl
 from jax.experimental.pallas import tpu as pltpu
@@ -18,7 +17,7 @@
 CAP = 20
 SPLIT = 4
 UNIT = CAP * SPLIT
-CHUNKS = 4
+CHUNKS = 2
 PAIR = 4
 MESH = pl.DeviceIdType.MESH
 
@@ -141,9 +140,12 @@
     c_wait(0)
     for k in range(1, far):
         z_forward(k)
-        attend_to(k - 1)
+    attend_to(0)
+    for k in range(1, far):
         y_forward(k)
         c_wait(k)
+        if k < far - 1:
+            attend_to(k)
     attend_to(far - 1)
 
     squares = jnp.zeros((tokens, 1), jnp.float32)
@@ -155,8 +157,9 @@
             squares = squares + jnp.sum(out * out, axis=1, keepdims=True)
             attended[:, column:column + HEAD_DIM] = out * gain[:, column:column + HEAD_DIM]
     stats[0] = jnp.zeros_like(stats[0])
-    stats[0, :, :EXPERTS] = jnp.dot(
-        attended[...], router[...], preferred_element_type=jnp.float32, precision=lax.Precision.HIGHEST
+    stats[0, :, :EXPERTS] = lax.dot_general(
+        attended[...], router[...], (((1,), (1,)), ((), ())), preferred_element_type=jnp.float32,
+        precision=lax.Precision.HIGHEST,
     )
     stats[1] = jnp.broadcast_to(squares, stats.shape[1:])
     swap = pltpu.make_async_remote_copy(
@@ -207,15 +210,15 @@
             pltpu.SemaphoreType.DMA((1,)),
         ],
         compiler_params=pltpu.CompilerParams(
-            collective_id=0, has_side_effects=True, vmem_limit_bytes=48 << 20
+            collective_id=0, has_side_effects=True, vmem_limit_bytes=63 << 20
         ),
         name="attend",
-    )(queries, keys, values, gain.reshape(1, -1), router)
+    )(queries, keys, values, gain.reshape(1, -1), router.T)
 
 
 def experts_kernel(
-    n, normed, logits, routes, order, order_t, w_gate, w_up, w_down, out_ref,
-    mix, gate_w, up_w, down_w, packed, disp, rows_x, gu_send, gu_own, gu_recv, hidden, parts, group_parts,
+    n, normed, logits, routes, w_gate, w_up, w_down, out_ref,
+    order, order_t, mix, gate_w, up_w, down_w, packed, disp, rows_x, gu_send, gu_own, gu_recv, hidden, parts, group_parts,
     back, returned, w_sem, own_sem, d_send, f_send, d_recv, x_send, x_recv, h_send, h_recv,
     g_send, g_recv, r_send, r_recv,
 ):
@@ -238,8 +241,7 @@
         load.start()
 
     def block_at(q):
-        pair = (b // 2 + 1) % 2 if q < 2 else b // 2
-        return pair * 2 + (b % 2 if q % 2 == (0 if q < 2 else 1) else 1 - b % 2)
+        return (b + 1 + q) % 2
 
     def expert_at(q, i, sign):
         return block_at(q) * block + (el + block + sign * i) % block
@@ -260,16 +262,20 @@
     tokens = normed.shape[0]
     f32 = jnp.float32
     lane = lax.broadcasted_iota(jnp.int32, (tokens, 128), 1)
-    picks = [(lane == routes[:, k:k + 1]).astype(f32) for k in range(TOP)]
-    earlier = (
-        lax.broadcasted_iota(jnp.int32, (tokens, tokens), 1) < lax.broadcasted_iota(jnp.int32, (tokens, tokens), 0)
-    )
+    down_at = lax.broadcasted_iota(jnp.int32, (tokens, tokens), 0)
+    across_at = lax.broadcasted_iota(jnp.int32, (tokens, tokens), 1)
+    named = lax.dot_general(
+        (down_at == across_at).astype(jnp.bfloat16), routes[...].astype(f32).astype(jnp.bfloat16),
+        (((1,), (1,)), ((), ())), preferred_element_type=f32,
+    )
+    picks = [(lane.astype(f32) == named[:, k:k + 1]).astype(f32) for k in range(TOP)]
+    earlier = across_at < down_at
     before = jnp.dot(
         earlier.astype(jnp.bfloat16), (picks[0] + picks[1]).astype(jnp.bfloat16), preferred_element_type=f32
     )
     chosen = [jnp.sum(pick * logits[...], axis=1, keepdims=True) for pick in picks]
     cells = [
-        routes[:, k:k + 1].astype(f32) * CAP + jnp.sum(picks[k] * before, axis=1, keepdims=True)
+        named[:, k:k + 1] * CAP + jnp.sum(picks[k] * before, axis=1, keepdims=True)
         for k in range(TOP)
     ]
     combine = [1.0 / (1.0 + jnp.exp(chosen[1 - k] - chosen[k])) for k in range(TOP)]
@@ -280,13 +286,7 @@
     cell = (unit * CAP + rest - column * CAP).astype(f32)
     hits = [cell == cells[k] for k in range(TOP)]
     placing = jnp.where(hits[0] | hits[1], 1.0, 0.0)
-    share = jnp.where(hits[0], combine[0], 0.0) + jnp.where(hits[1], combine[1], 0.0)
-    coarse = share.astype(jnp.bfloat16).astype(f32)
-    fine = share - coarse
     place = jnp.concatenate([jnp.where(column == c, placing, 0.0) for c in range(SPLIT)], axis=0)
-    for c in range(SPLIT):
-        mix[2 * c * tokens:(2 * c + 1) * tokens, :] = jnp.where(column == c, coarse, 0.0).astype(jnp.bfloat16)
-        mix[(2 * c + 1) * tokens:(2 * c + 2) * tokens, :] = jnp.where(column == c, fine, 0.0).astype(jnp.bfloat16)
     stacked = jnp.concatenate([normed[:, c * width:(c + 1) * width] for c in range(SPLIT)], axis=0)
     rows_out = lax.dot_general(
         place.astype(jnp.bfloat16), stacked, (((0,), (0,)), ((), ())), preferred_element_type=f32
@@ -321,6 +321,26 @@
             packed.at[e], disp.at[me], f_send.at[0, g - 1], d_recv.at[me],
             on_ctx(e * members + (j + g) % members),
         )
+
+    share = jnp.where(hits[0], combine[0], 0.0) + jnp.where(hits[1], combine[1], 0.0)
+    coarse = share.astype(jnp.bfloat16).astype(f32)
+    fine = share - coarse
+    for c in range(SPLIT):
+        mix[2 * c * tokens:(2 * c + 1) * tokens, :] = jnp.where(column == c, coarse, 0.0).astype(jnp.bfloat16)
+        mix[(2 * c + 1) * tokens:(2 * c + 2) * tokens, :] = jnp.where(column == c, fine, 0.0).astype(jnp.bfloat16)
+
+    side = PAIR * UNIT
+
+    def origin(spot):
+        split = (spot * 820) >> 16
+        rest = spot - split * UNIT
+        source = (rest * 3277) >> 16
+        return source * UNIT + split * CAP + rest - source * CAP
+
+    rows_at = lax.broadcasted_iota(jnp.int32, (side, side), 0)
+    columns_at = lax.broadcasted_iota(jnp.int32, (side, side), 1)
+    order[...] = jnp.where(columns_at == origin(rows_at), 1.0, 0.0).astype(jnp.bfloat16)
+    order_t[...] = jnp.where(rows_at == origin(columns_at), 1.0, 0.0).astype(jnp.bfloat16)
 
     def first_slot(q):
         return block_at(q) * block * members
@@ -454,13 +474,6 @@
     ff = w_gate.shape[1]
     chunk_rows = n * CAP // CHUNKS
     block = EXPERTS // CHUNKS
-    tall = np.arange(PAIR * UNIT)
-    column, rest = tall // (PAIR * CAP), tall % (PAIR * CAP)
-    origin = (rest // CAP) * UNIT + column * CAP + rest % CAP
-    perm = np.zeros((PAIR * UNIT, PAIR * UNIT), np.float32)
-    perm[tall, origin] = 1.0
-    order = jnp.asarray(perm, jnp.bfloat16)
-    order_t = jnp.asarray(perm.T, jnp.bfloat16)
     vmem = pl.BlockSpec(memory_space=pltpu.VMEM)
     any_spec = pl.BlockSpec(memory_space=pltpu.HBM)
     bf16 = jnp.bfloat16
@@ -469,9 +482,11 @@
     return pl.pallas_call(
         functools.partial(experts_kernel, n),
         out_shape=jax.ShapeDtypeStruct((tokens, wide), bf16),
-        in_specs=[vmem] * 5 + [any_spec] * 3,
+        in_specs=[vmem] * 3 + [any_spec] * 3,
         out_specs=vmem,
         scratch_shapes=[
+            pltpu.VMEM((PAIR * UNIT, PAIR * UNIT), bf16),
+            pltpu.VMEM((PAIR * UNIT, PAIR * UNIT), bf16),
             pltpu.VMEM((SPLIT * 2 * tokens, EXPERTS * UNIT), bf16),
             pltpu.VMEM(w_gate.shape, bf16),
             pltpu.VMEM(w_up.shape, bf16),
@@ -502,10 +517,10 @@
             dma((EXPERTS,)),
         ],
         compiler_params=pltpu.CompilerParams(
-            collective_id=1, has_side_effects=True, vmem_limit_bytes=60 << 20
+            collective_id=1, has_side_effects=True, vmem_limit_bytes=63 << 20
         ),
         name="experts",
-    )(normed, logits, routes, order, order_t, w_gate, w_up, w_down)
+    )(normed, logits, routes.T, w_gate, w_up, w_down)
 
 
 def on_device(queries, keys, values, gain, router, w_gate, w_up, w_down, routes):

time: 134 us -> 128 us (0.955)
  the two profiles are of different devices: /device:TPU:9 before, /device:TPU:4 now
where the time goes in v3:
time: 128 us; the launch traced here: 127 us
  Pallas kernels  124 us (97%)
  local copies, waits for them, and re-layouts  2.52 us (2%)
    pallas_call x1, Pallas kernels, run_experts(): pl.pallas_call(functools.partial(experts_kernel, n), out_shape=jax.ShapeD...  86.3 us
    pallas_call x1, Pallas kernels, attend(): pl.pallas_call(functools.partial(attend_kernel, n), out_shape=(jax.ShapeD...  37.8 us

profile of v3, /device:TPU:4, one launch (start us, length us, event | category | flops | bytes accessed | tf_op | source)
XLA Modules:
  0.0 127.3 jit_solution(2202261689473472144)
XLA Ops:
  0.6 37.8 %attend.1 = (bf16[64,3072]{1,0:T(8,128)(2,1)}, f32[64,128]{1,0:T(8,128)}) custom-call(bf16[64,3072]{1,0:T(8,128)(2,1)} %q_hbm.1, bf16[80,512]{1,0:T(8,128)(2,1)} %k_hbm.1, bf16[80,512]{1,0:T(8,128)(2,1)} %v_hbm.1, f32[1,3072]{1,0:T(1,128)} %bitcast.4, f32[8,3072]{1,0:T(8,128)} %bitcast.3), custom_call_target="tpu_custom_call" | custom-call | tf_op jit(solution)/shard_map/attend/pallas_call | solution.py:186
  38.5 0.0 copy-start
  38.5 86.3 %experts.1 = bf16[64,3072]{1,0:T(8,128)(2,1)} custom-call(bf16[64,3072]{1,0:T(8,128)(2,1)} %get-tuple-element.8.normed, f32[64,128]{1,0:T(8,128)} %get-tuple-element.5.logits, s32[2,64]{1,0:T(2,128)} %bitcast.5, bf16[3072,1024]{1,0:T(8,128)(2,1)} %w_gate.1, bf16[3072,1024]{1,0:T(8,128)(2,1)} %w_up.1, bf16[1024,3072]{1,0:T(8,128)(2,1)} %w_down.1), custom_call_target="tpu_custom_call" | custom-call | tf_op jit(solution)/shard_map/experts/pallas_call | solution.py:482
  124.8 0.0 copy-done
  124.8 0.7 copy.13
  125.6 1.8 %copy.14 = bf16[64,3072]{1,0:T(8,128)(2,1)} copy(bf16[64,3072]{1,0:T(8,128)(2,1)} %experts.1) | data formatting | bytes 786432
Async XLA Ops:
  38.5 86.4 %copy-start = (bf16[64,3072]{1,0:T(8,128)(2,1)S(1)}, bf16[64,3072]{1,0:T(8,128)(2,1)}, u32[]{:S(2)}) copy-start(bf16[64,3072]{1,0:T(8,128)(2,1)} %get-tuple-element.8.normed) | copy-start | bytes 1179652
